TPU v7x, 512 devices: a whole 4x8x8 slice. The times are simulated.
512 devices in a mesh: mem: 8 (over z_hi, core), grid: 64 (over y, x, z_lo).
Axes of the slice: x: 4, y: 8, z: 8 (z_hi: 4, z_lo: 2; z = z_hi * 2 + z_lo), core: 2. Of those that a mesh axis runs over, the one named last changes fastest.
Arguments:
- control: bfloat16 [32, 32, 384, 768], P('mem', None, 'grid'), may hold values from -6 to 6
- perturbation: bfloat16 [32, 32, 768, 384], P('mem', None, 'grid'), may hold values from -6 to 6
- vertical: bfloat16 [32, 32], replicated, may hold values from 0 to 1
- lat_counts: int32 [64], replicated, may hold values from 1 to 6, 361 in all
- lon_counts: int32 [64], replicated, may hold values from 1 to 12, 720 in all
Outputs:
- increment: float32 [32, 768, 384], P('mem', 'grid')
Inputs may be any that keep to these rules, and one draw needn't show every extreme that they name: Slab g holds its first lat_counts[g] latitude slots as real rows, numbered on from the slabs before it. Slab g holds its first lon_counts[g] longitude slots as real columns, numbered on from the slabs before it.
All inputs are finite; a program needn't handle non-finite values.
Results may differ from a plain program's by a relative error of at most 0.0067.
Values may be sent and summed in bfloat16 or wider, within the bound.
A program may use at most 64 MiB of HBM per device.

v0:
```python
import jax
import jax.numpy as jnp
from jax import lax
from jax.sharding import PartitionSpec as P

LAT = 361
LON = 720
LENGTH = 8
BAND = 48


def slot_table(counts, slot_count):
    devices = counts.shape[0]
    slot_ids = jnp.arange(devices * slot_count, dtype=jnp.int32)
    device_of = slot_ids // slot_count
    offset_in = slot_ids - device_of * slot_count
    offsets = jnp.cumsum(counts) - counts
    one_hot = device_of[:, None] == jnp.arange(devices, dtype=jnp.int32)[None, :]
    count_of = jnp.sum(jnp.where(one_hot, counts[None, :], 0), axis=1)
    start_of = jnp.sum(jnp.where(one_hot, offsets[None, :], 0), axis=1)
    return (start_of + offset_in, offset_in < count_of)


def pass_matrix(counts, slot_count, extent, periodic):
    position, usable = slot_table(counts, slot_count)
    lag = position[None, :] - position[:, None]
    if periodic:
        lag = jnp.where(lag < 0, lag + extent, lag)
    steps_f = jnp.arange(0, BAND + 1).astype(jnp.float32)
    normal_sum = jnp.sqrt(jnp.sum(jnp.exp(-2.0 * steps_f / LENGTH)))
    lag_f = lag.astype(jnp.float32)
    inside = (lag >= 0) & (lag <= BAND) & usable[:, None] & usable[None, :]
    weight = jnp.where(inside, jnp.exp(-lag_f / LENGTH) / normal_sum, 0.0)
    return weight.astype(jnp.bfloat16)


def per_device(control, perturbation, vertical, lat_counts, lon_counts):
    groups = lax.axis_size("grid")
    row_slots = control.shape[2]
    lon_pad = control.shape[3]
    col_slots = lon_pad // groups
    lon_matrix = pass_matrix(lon_counts, col_slots, LON, True)
    lat_matrix = pass_matrix(lat_counts, row_slots, LAT, False)
    smooth = jnp.dot(control.reshape(-1, lon_pad), lon_matrix, preferred_element_type=jnp.float32)
    smooth = smooth.astype(jnp.bfloat16).reshape(control.shape)
    columns = lax.all_to_all(smooth, "grid", split_axis=3, concat_axis=2, tiled=True)
    filtered = jnp.einsum(
        "mljc,ji->mlci", columns, lat_matrix, preferred_element_type=jnp.float32
    ).astype(jnp.bfloat16)
    mixed = jnp.einsum("kl,mlci->mkci", vertical, filtered, preferred_element_type=jnp.float32)
    partial_value = jnp.sum(mixed * perturbation.astype(jnp.float32), axis=0)
    summed = lax.psum(partial_value, "mem")
    level_share = partial_value.shape[0] // lax.axis_size("mem")
    return lax.dynamic_slice_in_dim(summed, lax.axis_index("mem") * level_share, level_share, 0)


def solution(mesh):
    in_specs = (P("mem", None, "grid", None), P("mem", None, "grid", None), P(), P(), P())
    out_specs = P("mem", "grid", None)
    return jax.shard_map(
        per_device, mesh=mesh, in_specs=in_specs, out_specs=out_specs, check_vma=False
    )
```

profile of v0, /device:TPU:2, one launch (start us, length us, event | category | flops | bytes accessed | tf_op | source)
XLA Modules:
  0.0 178.7 jit_solution(16469525209210127878)
XLA Ops:
  6.5 0.0 copy-start
  6.5 0.6 exponential_reduce_fusion
  7.2 0.7 copy.27
  7.9 0.1 reduce-window.18
  8.0 0.1 reduce
  8.1 0.7 sub.95
  8.8 0.8 select_reduce_fusion
  10.3 1.9 %copy.28 = bf16[4,32,6,768]{3,2,1,0:T(8,128)(2,1)S(1)} copy(bf16[4,32,6,768]{3,1,2,0:T(8,128)(2,1)} %param.5) | data formatting | bytes 2359296 | tf_op args[0]
  12.2 0.4 reshape.168
  12.7 2.8 %fusion.11 = bf16[768,768]{1,0:T(8,128)(2,1)} fusion(bf16[768,768]{1,0:T(8,128)(2,1)S(1)} %reshape.168, f32[]{:T(128)S(6)} %sqrt.4, s32[768]{0:T(1024)S(1)} %fusion.59, pred[768]{0:T(1024)(128)(4,1)S(1)} %fusion.58), kind=kOutput, calls=%fused_computation.13 | convolution fusion | flops 915406848 | bytes 2363140 | tf_op jit(solution)/shard_map/dot_general | solution.py:44
  15.5 2.2 %reshape.169 = bf16[4,32,6,768]{3,2,1,0:T(8,128)(2,1)S(1)} reshape(bf16[768,768]{1,0:T(8,128)(2,1)} %fusion.11) | data formatting | bytes 2359296 | tf_op jit(solution)/shard_map/reshape | solution.py:45
  17.7 4.6 %copy.29 = bf16[4,32,6,768]{1,0,2,3:T(4,128)(2,1)} copy(bf16[4,32,6,768]{3,2,1,0:T(8,128)(2,1)S(1)} %reshape.169) | data formatting | bytes 2359296 | tf_op jit(solution)/shard_map/reshape | solution.py:45
  22.3 8.1 %reshape.176 = bf16[64,2,4608]{2,1,0:T(2,128)(2,1)} reshape(bf16[768,6,4,32]{3,2,1,0:T(4,128)(2,1)} %bitcast.26) | data formatting | bytes 2359296
  30.4 0.0 copy-start.1
  30.4 12.6 %all-to-all-start = ((bf16[64,2,4608]{2,1,0:T(2,128)(2,1)}), bf16[64,2,4608]{2,1,0:T(2,128)(2,1)S(1)}, u32[]{:S(2)}, u32[]{:S(2)}) async-start(bf16[64,2,4608]{2,1,0:T(2,128)(2,1)} %reshape.176), calls=%async_computation | async-start | bytes 2359296 | tf_op jit(solution)/shard_map/all_to_all | solution.py:46
  43.0 0.0 all-reduce.2.cloned.1.call-start
  43.1 0.0 copy-done.1
  43.1 0.1 copy.32
  43.2 0.1 reduce-window.19
  43.3 0.1 reduce.1
  43.4 0.1 select_reduce_fusion.2
  43.6 30.2 %all-to-all-done = bf16[64,2,4608]{2,1,0:T(2,128)(2,1)S(1)} async-done(((bf16[64,2,4608]{2,1,0:T(2,128)(2,1)}), bf16[64,2,4608]{2,1,0:T(2,128)(2,1)S(1)}, u32[]{:S(2)}, u32[]{:S(2)}) %all-to-all-start) | async-done | bytes 1179680 | tf_op jit(solution)/shard_map/all_to_all | solution.py:46
  73.8 4.1 %reshape.177 = bf16[768,6,4,32]{3,2,1,0:T(4,128)(2,1)} reshape(bf16[64,2,4608]{2,1,0:T(2,128)(2,1)S(1)} %all-to-all-done) | data formatting | bytes 2359296
  77.8 0.0 copy-start.2
  77.8 6.2 %copy.31 = bf16[4,32,64,6,12]{1,0,4,3,2:T(4,128)(2,1)} copy(bf16[4,32,64,6,12]{1,0,3,4,2:T(4,128)(2,1)} %bitcast.27) | data formatting | bytes 2359296 | tf_op jit(solution)/shard_map/all_to_all | solution.py:46
  84.0 0.0 copy-done
  84.0 0.0 copy-done.2
  84.0 5.9 %fusion.2 = f32[32,12,384]{2,0,1:T(8,128)} fusion(bf16[4,32,12,384]{3,1,2,0:T(8,128)(2,1)S(1)} %copy-done.2, bf16[4,32,384,12]{1,0,3,2:T(4,128)(2,1)} %bitcast.28, f32[]{:T(128)S(6)} %sqrt.4, s32[384]{0:T(512)S(1)} %fusion.64, pred[384]{0:T(512)(128)(4,1)S(1)} %fusion.63, bf16[32,32]{1,0:T(8,128)(2,1)S(1)} %copy-done), kind=kOutput, calls=%fused_computation.4 | convolution fusion | flops 494714880 | bytes 2953092 | tf_op jit(solution)/shard_map/kl,mlci->mkci/dot_general | solution.py:50
  89.9 0.0 all-reduce.2.cloned.1.call-update
  90.0 80.3 %all-reduce.2.cloned.1.call-done = f32[32,12,384]{2,0,1:T(8,128)} async-done(((f32[32,12,384]{2,0,1:T(8,128)}), f32[32,12,384]{2,0,1:T(8,128)}) %all-reduce.2.cloned.1.call-update) | async-done | bytes 589840 | tf_op jit(solution)/shard_map/psum | solution.py:52
  170.3 1.6 constant_dynamic-slice_fusion
  (7 shorter events, 0.1 us)
Async XLA Ops:
  6.5 77.5 %copy-start = (bf16[32,32]{1,0:T(8,128)(2,1)S(1)}, bf16[32,32]{1,0:T(8,128)(2,1)}, u32[]{:S(2)}) copy-start(bf16[32,32]{1,0:T(8,128)(2,1)} %param.7) | copy-start | bytes 6148
  30.4 12.7 %copy-start.1 = (s32[64]{0:T(128)S(1)}, s32[64]{0:T(128)}, u32[]{:S(2)}) copy-start(s32[64]{0:T(128)} %param.8) | copy-start | bytes 772
  30.4 43.3 %all-to-all-start = ((bf16[64,2,4608]{2,1,0:T(2,128)(2,1)}), bf16[64,2,4608]{2,1,0:T(2,128)(2,1)S(1)}, u32[]{:S(2)}, u32[]{:S(2)}) async-start(bf16[64,2,4608]{2,1,0:T(2,128)(2,1)} %reshape.176), calls=%async_computation | async-start | bytes 2359296 | tf_op jit(solution)/shard_map/all_to_all | solution.py:46
  43.0 127.2 %all-reduce.2.cloned.1.call-start = ((), (), s32[]{:S(2)}) async-start(), calls=%async_computation.1 | async-start | bytes 1179648 | tf_op jit(solution)/shard_map/psum | solution.py:52
  77.8 6.2 %copy-start.2 = (bf16[4,32,12,384]{3,1,2,0:T(8,128)(2,1)S(1)}, bf16[4,32,12,384]{3,1,2,0:T(8,128)(2,1)}, u32[]{:S(2)}) copy-start(bf16[4,32,12,384]{3,1,2,0:T(8,128)(2,1)} %param.6) | copy-start | bytes 3538948
Sparse Core Ops, SparseCore 0:
  90.1 80.1 all-reduce.1
where the time goes:
time: 179 us
  waiting for transfers between devices  111 us (62%)
  local copies, waits for them, and re-layouts  30 us (17%)
  between operations  14.2 us (8%)
  starting transfers between devices  12.6 us (7%)
  matrix products  8.74 us (5%)
  other arithmetic  2.63 us (1%)
    psum x1, waiting for transfers between devices, per_device(): summed = lax.psum(partial_value, 'mem')  80.3 us
    all_to_all x1, waiting for transfers between devices, per_device(): lax.all_to_all(smooth, 'grid', split_axis=3, concat_axis=2, tiled=True)  30.2 us
    unnamed x9, local copies, waits for them, and re-layouts  14.2 us
    all_to_all x1, starting transfers between devices, per_device(): lax.all_to_all(smooth, 'grid', split_axis=3, concat_axis=2, tiled=True)  12.6 us
    reshape x2, local copies, waits for them, and re-layouts, per_device(): smooth = smooth.astype(jnp.bfloat16).reshape(control.shape)  6.78 us
    all_to_all x1, local copies, waits for them, and re-layouts, per_device(): lax.all_to_all(smooth, 'grid', split_axis=3, concat_axis=2, tiled=True)  6.17 us
    dot_general x1, matrix products, per_device(): jnp.einsum('kl,mlci->mkci', vertical, filtered, preferred_element_type=jn...  5.9 us
  transfers between devices with their start and end apart: 2, of which 2 were waited for; matrix products, arithmetic and copies ran while one was open for 0% of the time, Pallas kernels for 0%

commit v1 on v0

--- a/solution.py
+++ b/solution.py
@@ -49,7 +49,7 @@
     ).astype(jnp.bfloat16)
     mixed = jnp.einsum("kl,mlci->mkci", vertical, filtered, preferred_element_type=jnp.float32)
     partial_value = jnp.sum(mixed * perturbation.astype(jnp.float32), axis=0)
-    summed = lax.psum(partial_value, "mem")
+    summed = jnp.sum(lax.all_gather(partial_value, "mem"), axis=0)
     level_share = partial_value.shape[0] // lax.axis_size("mem")
     return lax.dynamic_slice_in_dim(summed, lax.axis_index("mem") * level_share, level_share, 0)
 

time: 179 us -> 163 us (0.911)
  the two profiles are of different devices: /device:TPU:2 before, /device:TPU:1 now
where the time goes in v1:
time: 163 us; the launch traced here: 162 us
  waiting for transfers between devices  91.4 us (56%)
  local copies, waits for them, and re-layouts  29.1 us (18%)
  between operations  14.2 us (9%)
  starting transfers between devices  13.3 us (8%)
  matrix products  8.75 us (5%)
  other arithmetic  5.46 us (3%)
    all_gather x1, waiting for transfers between devices, per_device(): summed = jnp.sum(lax.all_gather(partial_value, 'mem'), axis=0)  63.4 us
    all_to_all x1, waiting for transfers between devices, per_device(): lax.all_to_all(smooth, 'grid', split_axis=3, concat_axis=2, tiled=True)  28 us
    unnamed x9, local copies, waits for them, and re-layouts  14.2 us
    all_to_all x1, starting transfers between devices, per_device(): lax.all_to_all(smooth, 'grid', split_axis=3, concat_axis=2, tiled=True)  13.1 us
    reshape x2, local copies, waits for them, and re-layouts, per_device(): smooth = smooth.astype(jnp.bfloat16).reshape(control.shape)  6.78 us
    all_to_all x1, local copies, waits for them, and re-layouts, per_device(): lax.all_to_all(smooth, 'grid', split_axis=3, concat_axis=2, tiled=True)  6.17 us
    dot_general x1, matrix products, per_device(): jnp.einsum('kl,mlci->mkci', vertical, filtered, preferred_element_type=jn...  5.9 us
  transfers between devices with their start and end apart: 2, of which 2 were waited for; matrix products, arithmetic and copies ran while one was open for 0% of the time, Pallas kernels for 0%

profile of v1, /device:TPU:1, one launch (start us, length us, event | category | flops | bytes accessed | tf_op | source)
XLA Modules:
  0.0 162.1 jit_solution(14165979870529255176)
XLA Ops:
  6.5 0.0 copy-start
  6.5 0.6 exponential_reduce_fusion
  7.2 0.7 copy.27
  7.9 0.1 reduce-window.18
  8.0 0.1 reduce
  8.1 0.7 sub.95
  8.8 0.8 select_reduce_fusion
  10.3 1.9 %copy.28 = bf16[4,32,6,768]{3,2,1,0:T(8,128)(2,1)S(1)} copy(bf16[4,32,6,768]{3,1,2,0:T(8,128)(2,1)} %param.5) | data formatting | bytes 2359296 | tf_op args[0]
  12.2 0.4 reshape.168
  12.7 2.9 %fusion.11 = bf16[768,768]{1,0:T(8,128)(2,1)} fusion(bf16[768,768]{1,0:T(8,128)(2,1)S(1)} %reshape.168, f32[]{:T(128)S(6)} %sqrt.4, s32[768]{0:T(1024)S(1)} %fusion.59, pred[768]{0:T(1024)(128)(4,1)S(1)} %fusion.58), kind=kOutput, calls=%fused_computation.13 | convolution fusion | flops 915406848 | bytes 2363140 | tf_op jit(solution)/shard_map/dot_general | solution.py:44
  15.5 2.2 %reshape.169 = bf16[4,32,6,768]{3,2,1,0:T(8,128)(2,1)S(1)} reshape(bf16[768,768]{1,0:T(8,128)(2,1)} %fusion.11) | data formatting | bytes 2359296 | tf_op jit(solution)/shard_map/reshape | solution.py:45
  17.8 4.6 %copy.29 = bf16[4,32,6,768]{1,0,2,3:T(4,128)(2,1)} copy(bf16[4,32,6,768]{3,2,1,0:T(8,128)(2,1)S(1)} %reshape.169) | data formatting | bytes 2359296 | tf_op jit(solution)/shard_map/reshape | solution.py:45
  22.3 8.1 %reshape.177 = bf16[64,2,4608]{2,1,0:T(2,128)(2,1)} reshape(bf16[768,6,4,32]{3,2,1,0:T(4,128)(2,1)} %bitcast.27) | data formatting | bytes 2359296
  30.5 0.0 copy-start.1
  30.5 13.1 %all-to-all-start = ((bf16[64,2,4608]{2,1,0:T(2,128)(2,1)}), bf16[64,2,4608]{2,1,0:T(2,128)(2,1)S(1)}, u32[]{:S(2)}, u32[]{:S(2)}) async-start(bf16[64,2,4608]{2,1,0:T(2,128)(2,1)} %reshape.177), calls=%async_computation | async-start | bytes 2359296 | tf_op jit(solution)/shard_map/all_to_all | solution.py:46
  43.5 0.2 all-gather.3.cloned.1.call-start
  43.7 0.0 copy-done.1
  43.8 0.1 copy.32
  43.9 0.1 reduce-window.19
  43.9 0.1 reduce.1
  44.1 0.1 select_reduce_fusion.2
  44.2 28.0 %all-to-all-done = bf16[64,2,4608]{2,1,0:T(2,128)(2,1)S(1)} async-done(((bf16[64,2,4608]{2,1,0:T(2,128)(2,1)}), bf16[64,2,4608]{2,1,0:T(2,128)(2,1)S(1)}, u32[]{:S(2)}, u32[]{:S(2)}) %all-to-all-start) | async-done | bytes 1179680 | tf_op jit(solution)/shard_map/all_to_all | solution.py:46
  72.2 4.1 %reshape.178 = bf16[768,6,4,32]{3,2,1,0:T(4,128)(2,1)} reshape(bf16[64,2,4608]{2,1,0:T(2,128)(2,1)S(1)} %all-to-all-done) | data formatting | bytes 2359296
  76.3 0.0 copy-start.2
  76.3 6.2 %copy.31 = bf16[4,32,64,6,12]{1,0,4,3,2:T(4,128)(2,1)} copy(bf16[4,32,64,6,12]{1,0,3,4,2:T(4,128)(2,1)} %bitcast.28) | data formatting | bytes 2359296 | tf_op jit(solution)/shard_map/all_to_all | solution.py:46
  82.5 0.0 copy-done
  82.5 0.0 copy-done.2
  82.5 5.9 %fusion.2 = f32[32,12,384]{2,0,1:T(8,128)} fusion(bf16[4,32,12,384]{3,1,2,0:T(8,128)(2,1)S(1)} %copy-done.2, bf16[4,32,384,12]{1,0,3,2:T(4,128)(2,1)} %bitcast.29, f32[]{:T(128)S(6)} %sqrt.4, s32[384]{0:T(512)S(1)} %fusion.64, pred[384]{0:T(512)(128)(4,1)S(1)} %fusion.63, bf16[32,32]{1,0:T(8,128)(2,1)S(1)} %copy-done), kind=kOutput, calls=%fused_computation.4 | convolution fusion | flops 494714880 | bytes 2953092 | tf_op jit(solution)/shard_map/kl,mlci->mkci/dot_general | solution.py:50
  88.4 0.0 all-gather.3.cloned.1.call-update
  88.4 63.4 %all-gather.3.cloned.1.call-done = f32[256,12,384]{2,0,1:T(8,128)} async-done(((f32[32,12,384]{2,0,1:T(8,128)}), f32[256,12,384]{2,0,1:T(8,128)}) %all-gather.3.cloned.1.call-update) | async-done | bytes 4718608 | tf_op jit(solution)/shard_map/all_gather | solution.py:52
  151.8 2.8 %reduce_sum.73 = f32[32,12,384]{2,0,1:T(8,128)S(1)} reduce(f32[8,32,12,384]{3,1,0,2:T(8,128)} %bitcast.30, f32[]{:T(128)} %constant.49.clone.1), dimensions={0}, to_apply=%region_8.9 | reduce | flops 1032192 | bytes 5308420 | tf_op jit(solution)/shard_map/reduce_sum | solution.py:52
  154.6 0.7 constant_dynamic-slice_fusion
  (7 shorter events, 0.1 us)
Async XLA Ops:
  6.5 75.9 %copy-start = (bf16[32,32]{1,0:T(8,128)(2,1)S(1)}, bf16[32,32]{1,0:T(8,128)(2,1)}, u32[]{:S(2)}) copy-start(bf16[32,32]{1,0:T(8,128)(2,1)} %param.7) | copy-start | bytes 6148
  30.5 13.3 %copy-start.1 = (s32[64]{0:T(128)S(1)}, s32[64]{0:T(128)}, u32[]{:S(2)}) copy-start(s32[64]{0:T(128)} %param.8) | copy-start | bytes 772
  30.5 41.8 %all-to-all-start = ((bf16[64,2,4608]{2,1,0:T(2,128)(2,1)}), bf16[64,2,4608]{2,1,0:T(2,128)(2,1)S(1)}, u32[]{:S(2)}, u32[]{:S(2)}) async-start(bf16[64,2,4608]{2,1,0:T(2,128)(2,1)} %reshape.177), calls=%async_computation | async-start | bytes 2359296 | tf_op jit(solution)/shard_map/all_to_all | solution.py:46
  43.5 108.3 %all-gather.3.cloned.1.call-start = ((), (), s32[]{:S(2)}) async-start(), calls=%async_computation.1 | async-start | bytes 5308416 | tf_op jit(solution)/shard_map/all_gather | solution.py:52
  76.3 6.2 %copy-start.2 = (bf16[4,32,12,384]{3,1,2,0:T(8,128)(2,1)S(1)}, bf16[4,32,12,384]{3,1,2,0:T(8,128)(2,1)}, u32[]{:S(2)}) copy-start(bf16[4,32,12,384]{3,1,2,0:T(8,128)(2,1)} %param.6) | copy-start | bytes 3538948
Sparse Core Ops, SparseCore 0:
  88.5 63.2 all-gather.2

commit v2 on v0

--- a/solution.py
+++ b/solution.py
@@ -43,7 +43,10 @@
     lat_matrix = pass_matrix(lat_counts, row_slots, LAT, False)
     smooth = jnp.dot(control.reshape(-1, lon_pad), lon_matrix, preferred_element_type=jnp.float32)
     smooth = smooth.astype(jnp.bfloat16).reshape(control.shape)
-    columns = lax.all_to_all(smooth, "grid", split_axis=3, concat_axis=2, tiled=True)
+    columns = jnp.concatenate(
+        lax.all_to_all(jnp.stack(jnp.split(smooth, lax.axis_size("grid"), axis=3)), "grid", 0, 0),
+        axis=2,
+    )
     filtered = jnp.einsum(
         "mljc,ji->mlci", columns, lat_matrix, preferred_element_type=jnp.float32
     ).astype(jnp.bfloat16)

time: 179 us -> 244 us (1.36)
  local copies, waits for them, and re-layouts: 30 us -> 94.4 us
    unnamed x9 -> x72, local copies, waits for them, and re-layouts: 14.2 us -> 67.2 us
    another operation x2 -> x4, local copies, waits for them, and re-layouts: 0.84 us -> 22.8 us  [the longest x2 22 us: per_device(): jnp.stack(jnp.split(smooth, lax.axis_size('grid'), axis=3))]
    all_to_all x1 -> x0, local copies, waits for them, and re-layouts: 6.17 us -> none  [per_device(): lax.all_to_all(smooth, 'grid', split_axis=3, concat_axis=2, tiled=True)]
    reshape x2 -> x1, local copies, waits for them, and re-layouts: 6.78 us -> 2.41 us  [per_device(): smooth = smooth.astype(jnp.bfloat16).reshape(control.shape)]
where the time goes in v2:
time: 244 us; the launch traced here: 243 us
  waiting for transfers between devices  111 us (45%)
  local copies, waits for them, and re-layouts  94.4 us (39%)
  between operations  14.2 us (6%)
  starting transfers between devices  12.5 us (5%)
  matrix products  8.71 us (4%)
  other arithmetic  2.63 us (1%)
    psum x1, waiting for transfers between devices, per_device(): summed = lax.psum(partial_value, 'mem')  80.4 us
    unnamed x72, local copies, waits for them, and re-layouts  67.2 us
    all_to_all x1, waiting for transfers between devices, per_device(): lax.all_to_all(jnp.stack(jnp.split(smooth, lax.axis_size('grid'), axis=3)...  30.2 us
    another operation x2, local copies, waits for them, and re-layouts, per_device(): jnp.stack(jnp.split(smooth, lax.axis_size('grid'), axis=3))  22 us
    all_to_all x1, starting transfers between devices, per_device(): lax.all_to_all(jnp.stack(jnp.split(smooth, lax.axis_size('grid'), axis=3)...  12.5 us
    dot_general x1, matrix products, per_device(): jnp.einsum('kl,mlci->mkci', vertical, filtered, preferred_element_type=jn...  5.87 us
  transfers between devices with their start and end apart: 2, of which 2 were waited for; matrix products, arithmetic and copies ran while one was open for 0% of the time, Pallas kernels for 0%

profile of v2, /device:TPU:2, one launch (start us, length us, event | category | flops | bytes accessed | tf_op | source)
XLA Modules:
  0.0 243.1 jit_solution(762742676908442568)
XLA Ops:
  10.3 1.9 copy.82
  12.7 2.8 %fusion.11 = bf16[768,768]{1,0:T(8,128)(2,1)} fusion(bf16[768,768]{1,0:T(8,128)(2,1)S(1)} %reshape.174, f32[]{:T(128)S(6)} %sqrt.4, s32[768]{0:T(1024)S(1)} %fusion.123, pred[768]{0:T(1024)(128)(4,1)S(1)} %fusion.122), kind=kOutput, calls=%fused_computation.13 | convolution fusion | flops 915406848 | bytes 2363140 | tf_op jit(solution)/shard_map/dot_general | solution.py:44
  15.5 2.4 reshape.175
  18.7 0.8 fusion.116
  19.5 0.8 fusion.115
  20.3 0.9 fusion.114
  21.2 0.9 fusion.113
  22.1 0.9 fusion.112
  22.9 0.8 fusion.111
  23.8 0.8 fusion.110
  24.6 0.9 fusion.109
  25.5 0.8 fusion.108
  26.3 0.8 fusion.107
  27.1 0.9 fusion.106
  28.0 0.9 fusion.105
  28.9 0.8 fusion.104
  30.6 0.8 fusion.102
  32.2 0.8 fusion.100
  33.1 0.8 fusion.99
  33.9 0.9 fusion.98
  34.8 0.8 fusion.97
  35.6 0.9 fusion.96
  36.5 0.8 fusion.95
  37.3 0.8 fusion.94
  38.2 0.8 fusion.93
  39.0 0.8 fusion.92
  39.9 0.9 fusion.91
  40.7 0.9 fusion.90
  41.6 0.8 fusion.89
  44.1 0.9 fusion.86
  45.7 0.8 fusion.84
  46.5 0.9 fusion.83
  47.4 0.9 fusion.82
  48.3 0.8 fusion.81
  49.1 0.9 fusion.80
  50.0 0.9 fusion.79
  50.8 0.9 fusion.78
  51.7 0.9 fusion.77
  52.5 0.9 fusion.76
  53.4 0.9 fusion.75
  55.1 0.8 fusion.73
  56.7 0.8 fusion.71
  57.6 0.9 fusion.70
  58.4 0.8 fusion.69
  59.3 0.8 fusion.68
  60.1 0.9 fusion.67
  61.0 0.8 fusion.66
  64.3 0.8 fusion.62
  65.2 0.8 fusion.61
  66.0 0.9 fusion.60
  66.9 0.9 fusion.59
  67.7 0.8 fusion.58
  68.6 0.8 fusion.57
  69.4 0.8 fusion.56
  70.3 0.8 fusion.55
  71.1 0.8 fusion.54
  72.0 21.1 %copy.83 = bf16[64,4,32,6,12]{2,1,4,3,0:T(4,128)(2,1)} copy(bf16[64,4,32,6,12]{4,3,2,1,0:T(8,128)(2,1)} %fusion.54) | data formatting | bytes 2359296 | tf_op jit(solution)/shard_map/stack | solution.py:47
  93.1 8.1 %reshape.184 = bf16[64,2,4608]{2,1,0:T(2,128)(2,1)} reshape(bf16[64,6,12,4,32]{4,3,2,1,0:T(4,128)(2,1)} %bitcast.281) | data formatting | bytes 2359296
  101.2 12.5 %all-to-all-start = ((bf16[64,2,4608]{2,1,0:T(2,128)(2,1)}), bf16[64,2,4608]{2,1,0:T(2,128)(2,1)S(1)}, u32[]{:S(2)}, u32[]{:S(2)}) async-start(bf16[64,2,4608]{2,1,0:T(2,128)(2,1)} %reshape.184), calls=%async_computation | async-start | bytes 2359296 | tf_op jit(solution)/shard_map/all_to_all | solution.py:47
  114.2 30.2 %all-to-all-done = bf16[64,2,4608]{2,1,0:T(2,128)(2,1)S(1)} async-done(((bf16[64,2,4608]{2,1,0:T(2,128)(2,1)}), bf16[64,2,4608]{2,1,0:T(2,128)(2,1)S(1)}, u32[]{:S(2)}, u32[]{:S(2)}) %all-to-all-start) | async-done | bytes 1179680 | tf_op jit(solution)/shard_map/all_to_all | solution.py:47
  144.4 4.0 %reshape.185 = bf16[64,6,12,4,32]{4,3,2,1,0:T(4,128)(2,1)} reshape(bf16[64,2,4608]{2,1,0:T(2,128)(2,1)S(1)} %all-to-all-done) | data formatting | bytes 2359296
  148.4 5.9 %fusion.2 = f32[32,12,384]{2,0,1:T(8,128)} fusion(bf16[4,32,12,384]{3,1,2,0:T(8,128)(2,1)S(1)} %copy-done.2, bf16[4,32,384,12]{1,0,3,2:T(4,128)(2,1)} %bitcast.282, f32[]{:T(128)S(6)} %sqrt.4, s32[384]{0:T(512)S(1)} %fusion.128, pred[384]{0:T(512)(128)(4,1)S(1)} %fusion.127, bf16[32,32]{1,0:T(8,128)(2,1)S(1)} %copy-done), kind=kOutput, calls=%fused_computation.4 | convolution fusion | flops 494714880 | bytes 2953092 | tf_op jit(solution)/shard_map/kl,mlci->mkci/dot_general | solution.py:53
  154.3 80.4 %all-reduce.2.cloned.1.call-done = f32[32,12,384]{2,0,1:T(8,128)} async-done(((f32[32,12,384]{2,0,1:T(8,128)}), f32[32,12,384]{2,0,1:T(8,128)}) %all-reduce.2.cloned.1.call-update) | async-done | bytes 589840 | tf_op jit(solution)/shard_map/psum | solution.py:55
  234.7 1.6 constant_dynamic-slice_fusion
  (37 shorter events, 12.9 us)
Async XLA Ops:
  6.5 141.9 %copy-start = (bf16[32,32]{1,0:T(8,128)(2,1)S(1)}, bf16[32,32]{1,0:T(8,128)(2,1)}, u32[]{:S(2)}) copy-start(bf16[32,32]{1,0:T(8,128)(2,1)} %param.7) | copy-start | bytes 6148
  66.0 47.7 %copy-start.1 = (s32[64]{0:T(128)S(1)}, s32[64]{0:T(128)}, u32[]{:S(2)}) copy-start(s32[64]{0:T(128)} %param.8) | copy-start | bytes 772
  72.0 76.4 %copy-start.2 = (bf16[4,32,12,384]{3,1,2,0:T(8,128)(2,1)S(1)}, bf16[4,32,12,384]{3,1,2,0:T(8,128)(2,1)}, u32[]{:S(2)}) copy-start(bf16[4,32,12,384]{3,1,2,0:T(8,128)(2,1)} %param.6) | copy-start | bytes 3538948
  101.2 43.2 %all-to-all-start = ((bf16[64,2,4608]{2,1,0:T(2,128)(2,1)}), bf16[64,2,4608]{2,1,0:T(2,128)(2,1)S(1)}, u32[]{:S(2)}, u32[]{:S(2)}) async-start(bf16[64,2,4608]{2,1,0:T(2,128)(2,1)} %reshape.184), calls=%async_computation | async-start | bytes 2359296 | tf_op jit(solution)/shard_map/all_to_all | solution.py:47
  113.7 121.0 %all-reduce.2.cloned.1.call-start = ((), (), s32[]{:S(2)}) async-start(), calls=%async_computation.1 | async-start | bytes 1179648 | tf_op jit(solution)/shard_map/psum | solution.py:55
Sparse Core Ops, SparseCore 0:
  154.4 80.2 all-reduce.1
